TPU v7x, 32 devices: a whole 2x2x4 slice. The times are simulated.
32 devices in a mesh: row: 4 (over x, core), col: 8 (over z, y).
Axes of the slice: x: 2, y: 2, z: 4, core: 2. Of those that a mesh axis runs over, the one named last changes fastest.
Arguments:
- vectors: float32 [32768, 128], P(('col', 'row')), may hold values from -6 to 6
- tile_values: bfloat16 [4, 8, 22, 512, 512], P('row', 'col'), may hold values from 0 to 1
- tile_rows: int32 [4, 8, 22], P('row', 'col'), may hold values from 0 to 15, as said below
- tile_cols: int32 [4, 8, 22], P('row', 'col'), may hold values from 0 to 7
- tile_count: int32 [4, 8], P('row', 'col'), may hold values from 1 to 22, as said below
- degrees: int32 [32768], replicated, may hold values from 16 to 255
Outputs:
- result: float32 [32768, 128], P(('row', 'col'))
Inputs may be any that keep to these rules, and one draw needn't show every extreme that they name: `tile_rows`: within one device no two slots name the same pair of tile row and tile column. `tile_count`: some device has all 22 slots live.
All inputs are finite; a program needn't handle non-finite values.
Results may differ from a plain program's by a relative error of at most 0.0003.
Values sent between devices are 32-bit elements; how exact they have to be, the bound alone decides.
A program may use at most 128 MiB of HBM per device.

v0:
```python
import functools

import jax
import jax.numpy as jnp
from jax import lax
from jax.experimental import pallas as pl
from jax.experimental.pallas import tpu as pltpu
from jax.sharding import PartitionSpec as P

MESH = pl.DeviceIdType.MESH


def inner_size(col_count):
    inner = 1
    while inner * inner * 4 <= col_count and col_count % (inner * 2) == 0:
        inner *= 2
    return inner


def kernel(
    dims,
    rows_s, cols_s, count_s, vec_ref, deg_ref, tiles_hbm, out_ref,
    tiles_v, gath, split_v, sums, inb, outb, zb, yb, prev_s, last_s,
    tile_sem, vec_sem, d_send, d_recv, m_send, m_recv, f_send, f_recv,
    i_send, i_recv, o_send, o_recv, z_send, z_recv, y_send, y_recv,
):
    R, A, B, piece, width, side, slots = dims
    C = A * B
    tpp = piece // side
    chips = R // 2
    me_row = lax.axis_index("row")
    me_col = lax.axis_index("col")
    chip, core = me_row // 2, me_row % 2
    mate = chip * 2 + (1 - core)
    a, b = me_col // B, me_col % B
    lanes = 128

    tile_copy = pltpu.make_async_copy(tiles_hbm.at[0, 0], tiles_v, tile_sem)
    tile_copy.start()

    def rdma(src, dst, ssem, rsem, where):
        return pltpu.make_async_remote_copy(
            src_ref=src, dst_ref=dst, send_sem=ssem, recv_sem=rsem,
            device_id=where, device_id_type=MESH,
        )

    barrier = pltpu.get_barrier_semaphore()

    def greet(where):
        pl.semaphore_signal(barrier, inc=1, device_id=where, device_id_type=MESH)

    greet({"row": mate})
    for j in range(1, chips):
        greet({"row": lax.rem(chip + j, chips) * 2 + core})
    conds = []
    if B > 1:
        conds += [(b > 0, me_col - 1), (b < B - 1, me_col + 1)]
    if A > 1:
        conds += [(a > 0, me_col - B), (a < A - 1, me_col + B)]
    for cond, other in conds:
        @pl.when(cond)
        def _(other=other):
            greet({"col": other})
    peers = jnp.int32(chips)
    for cond, other in conds:
        peers = peers + jnp.where(cond, 1, 0)
    pl.semaphore_wait(barrier, peers)

    def part(c):
        return pl.ds(c * side, side)

    directs, mates, forwards = {}, [], {}
    for c in range(tpp):
        for j in range(1, chips):
            dst = lax.rem(chip + j, chips) * 2 + core
            cp = rdma(vec_ref.at[part(c)], gath.at[me_row, part(c)],
                      d_send.at[j - 1, c], d_recv.at[j - 1, c], {"row": dst})
            cp.start()
            directs[j, c] = cp
    for c in range(tpp):
        cp = rdma(vec_ref.at[part(c)], gath.at[me_row, part(c)],
                  m_send.at[c], m_recv.at[c], {"row": mate})
        cp.start()
        mates.append(cp)

    vec_copy = pltpu.make_async_copy(vec_ref, gath.at[me_row], vec_sem)
    vec_copy.start()

    count = count_s[0, 0]

    def link(k, _):
        rk = rows_s[0, 0, k]
        v = jnp.int32(slots)
        for j in range(slots):
            v = jnp.where((rows_s[0, 0, j] == rk) & (j < k), j, v)
        prev_s[k] = v
        return 0

    lax.fori_loop(0, slots, link, 0)

    def ends(r, _):
        v = jnp.int32(slots)
        for j in range(slots):
            v = jnp.where((rows_s[0, 0, j] == r) & (j < count), j, v)
        last_s[r] = v
        return 0

    lax.fori_loop(0, C * tpp, ends, 0)
    sums[slots] = jnp.zeros((side, width), jnp.float32)

    def factors(first):
        d = deg_ref[pl.ds(first, 1), :].astype(jnp.float32)
        return jnp.broadcast_to(lax.rsqrt(d), (lanes, lanes)).T

    col_first = me_col * (R * piece // lanes)

    def scale(get, r, c):
        def step(q, _):
            f = factors(col_first + (r * piece + c * side) // lanes + q)
            x = get(pl.ds(c * side + q * lanes, lanes)) * f
            hi = x.astype(jnp.bfloat16)
            lo = (x - hi.astype(jnp.float32)).astype(jnp.bfloat16)
            at = pl.ds(pl.multiple_of(q * lanes, lanes), lanes)
            split_v[r * tpp + c, at, :width] = hi
            split_v[r * tpp + c, at, width:] = lo
            return 0

        lax.fori_loop(0, side // lanes, step, 0)

    def landed(r, c, ssem, rsem):
        rdma(gath.at[r, part(c)], gath.at[r, part(c)], ssem, rsem, {"row": mate}).wait_recv()

    vec_copy.wait()
    for c in range(tpp):
        scale(lambda s: gath[me_row, s, :], me_row, c)
    for c in range(tpp):
        landed(mate, c, m_send.at[c], m_recv.at[c])
        scale(lambda s: gath[mate, s, :], mate, c)
    for c in range(tpp):
        for j in range(1, chips):
            src = lax.rem(chip - j + chips, chips) * 2 + core
            landed(src, c, d_send.at[j - 1, c], d_recv.at[j - 1, c])
            cp = rdma(gath.at[src, part(c)], gath.at[src, part(c)],
                      f_send.at[j - 1, c], f_recv.at[j - 1, c], {"row": mate})
            cp.start()
            forwards[j, c] = cp
            scale(lambda s, src=src: gath[src, s, :], src, c)
    for c in range(tpp):
        for j in range(1, chips):
            src = lax.rem(chip - j + chips, chips) * 2 + (1 - core)
            landed(src, c, f_send.at[j - 1, c], f_recv.at[j - 1, c])
            scale(lambda s, src=src: gath[src, s, :], src, c)

    tile_copy.wait()

    def products(lo, n):
        def product(k, _):
            both = jnp.dot(tiles_v[k, lo:lo + n], split_v[cols_s[0, 0, k]],
                           preferred_element_type=jnp.float32)
            old = sums[prev_s[k], lo:lo + n]
            sums[k, lo:lo + n] = both[:, :width] + both[:, width:] + old
            return 0

        lax.fori_loop(0, slots, product, 0, unroll=True)

    order = sorted_table(A)
    cut = side - zb.shape[2]
    tail = (tpp - 1) * side + cut
    tail_rows = side - cut
    early = [(u, u * tail_rows, cut, tail_rows) for u in range(tpp - 1)]
    late_at = (tpp - 1) * tail_rows
    late = [(u, late_at + u * cut, 0, cut) for u in range(tpp)]
    spans = [(late_at, tpp * cut, late)]
    if early:
        spans = [(0, late_at, early)] + spans

    def pick(s):
        v = jnp.int32(order[0][s])
        for i in range(1, A):
            v = jnp.where(a == i, order[i][s], v)
        return v

    def own(d, t, u, lo, n):
        return sums[last_s[(d * B + t) * tpp + u], lo:lo + n]

    def own_tail(d, t):
        return sums[last_s[(d * B + t) * tpp + tpp - 1], cut:]

    def line(pos, size, stride, dist, action):
        for right in (True, False):
            t = pos + dist if right else pos - dist
            slot = t + 1 if right else t
            to = me_col + stride if right else me_col - stride
            more = pos > 0 if right else pos < size - 1

            @pl.when((t < size) if right else (t >= 0))
            def _(t=t, slot=slot, to=to, more=more):
                action(t, slot, to, more, dist < size - 1)

    def add_and_send(cp, more, can, store):
        if can:
            @pl.when(more)
            def _():
                cp.wait_recv()
                store(True)

            @pl.when(jnp.logical_not(more))
            def _():
                store(False)
        else:
            store(False)
        cp.start()

    def arrive(pos, size, ref, ssem, rsem, fold):
        if size > 1:
            for cond, slot in ((pos > 0, pos + 1), (pos < size - 1, pos)):
                @pl.when(cond)
                def _(slot=slot):
                    rdma(ref(slot), ref(slot), ssem(slot), rsem(slot), {"row": mate}).wait_recv()
        if size > 2:
            @pl.when((pos > 0) & (pos < size - 1))
            def _():
                fold(pos + 1, pos)

    near = jnp.where(b > 0, b + 1, 0)
    near_a = jnp.where(a > 0, a + 1, 0)

    def inner_copy(h, d, slot, to):
        at = inb.at[d, slot, pl.ds(*spans[h][:2])]
        return rdma(at, at, i_send.at[h, d, slot], i_recv.at[h, d, slot], {"col": to})

    def inner_send(h, d):
        def action(t, slot, to, more, can):
            def store(add):
                for u, at, lo, n in spans[h][2]:
                    rows = pl.ds(at, n)
                    v = own(d, t, u, lo, n)
                    inb[d, slot, rows] = inb[d, slot, rows] + v if add else v

            add_and_send(inner_copy(h, d, slot, to), more, can, store)
        return action

    def inner_done(h, d):
        rows = pl.ds(*spans[h][:2])

        def fold(x, y):
            inb[d, x, rows] = inb[d, x, rows] + inb[d, y, rows]

        arrive(b, B, lambda q: inb.at[d, q, rows], lambda q: i_send.at[h, d, q],
               lambda q: i_recv.at[h, d, q], fold)

    def here(d, u, at, lo, n):
        v = own(d, b, u, lo, n)
        if B > 1:
            v = v + inb[d, near, pl.ds(at, n)]
        return v

    def outer_copy(h, s):
        d = pick(s)
        right = d > a
        slot = jnp.where(right, d + 1, d)
        to = jnp.where(right, me_col + B, me_col - B)
        at = outb.at[slot, pl.ds(*spans[h][:2])]
        return d, right, slot, rdma(at, at, o_send.at[h, slot], o_recv.at[h, slot], {"col": to})

    def outer_step(h, s):
        d, right, slot, cp = outer_copy(h, s)
        inner_done(h, d)
        more = (right & (a > 0)) | (jnp.logical_not(right) & (a < A - 1))

        def store(add):
            for u, at, lo, n in spans[h][2]:
                rows = pl.ds(at, n)
                v = here(d, u, at, lo, n)
                outb[slot, rows] = outb[slot, rows] + v if add else v

        add_and_send(cp, more, True, store)

    def zcopy(slot, to):
        return rdma(zb.at[slot], zb.at[slot], z_send.at[slot], z_recv.at[slot], {"col": to})

    def zsend(d, slot, to, more, can):
        def store(add):
            for t in range(B):
                v = own_tail(d, t)
                zb[slot, t] = zb[slot, t] + v if add else v

        add_and_send(zcopy(slot, to), more, can, store)

    def zhere(t):
        v = own_tail(a, t)
        if A > 1:
            v = v + zb[near_a, t]
        return v

    def ycopy(slot, to):
        return rdma(yb.at[slot], yb.at[slot], y_send.at[slot], y_recv.at[slot], {"col": to})

    def ysend(t, slot, to, more, can):
        def store(add):
            v = zhere(t)
            yb[slot] = yb[slot] + v if add else v

        add_and_send(ycopy(slot, to), more, can, store)

    def zfold(x, y):
        zb[x] = zb[x] + zb[y]

    def yfold(x, y):
        yb[x] = yb[x] + yb[y]

    def tail_turn():
        arrive(a, A, lambda q: zb.at[q], lambda q: z_send.at[q], lambda q: z_recv.at[q], zfold)
        for dist in range(B - 1, 0, -1):
            line(b, B, 1, dist, ysend)

    def inner_all(h):
        for s in range(A):
            for dist in range(B - 1, 0, -1):
                line(b, B, 1, dist, inner_send(h, pick(s)))

    products(cut, tail_rows)
    if A > 1:
        line(a, A, B, A - 1, zsend)
    if early:
        inner_all(0)
    products(0, cut)
    inner_all(len(spans) - 1)
    for dist in range(A - 2, 1, -1):
        line(a, A, B, dist, zsend)
    turn = (len(spans) - 1, 0)
    for h in range(len(spans)):
        for s in range(A - 1):
            outer_step(h, s)
            if (h, s) == (0, 0) and A > 2:
                line(a, A, B, 1, zsend)
            if (h, s) == turn:
                tail_turn()
    if A == 1:
        tail_turn()

    for h in range(len(spans)):
        inner_done(h, a)
        first, rows, parts = spans[h]
        if A > 1:
            for cond, slot in ((a > 0, a + 1), (a < A - 1, a)):
                @pl.when(cond)
                def _(slot=slot, h=h, first=first, rows=rows):
                    at = outb.at[slot, pl.ds(first, rows)]
                    rdma(at, at, o_send.at[h, slot], o_recv.at[h, slot],
                         {"row": mate}).wait_recv()
        if A > 2:
            @pl.when((a > 0) & (a < A - 1))
            def _(first=first, rows=rows):
                at = pl.ds(first, rows)
                outb[a + 1, at] = outb[a + 1, at] + outb[a, at]
        for u, at, lo, n in parts:
            v = here(a, u, at, lo, n)
            if A > 1:
                v = v + outb[near_a, pl.ds(at, n)]
            out_ref[pl.ds(u * side + lo, n), :] = v
    arrive(b, B, lambda q: yb.at[q], lambda q: y_send.at[q], lambda q: y_recv.at[q], yfold)
    last = zhere(b)
    if B > 1:
        last = last + yb[near]
    out_ref[pl.ds(tail, tail_rows), :] = last
    out_first = (me_row * C + me_col) * (piece // lanes)
    for q in range(piece // lanes):
        at = pl.ds(q * lanes, lanes)
        out_ref[at, :] = out_ref[at, :] * factors(out_first + q)

    for group in (directs.values(), mates, forwards.values()):
        for cp in group:
            cp.wait_send()
    for dist in range(A - 1, 0, -1):
        line(a, A, B, dist, lambda t, slot, to, *rest: zcopy(slot, to).wait_send())
    for dist in range(B - 1, 0, -1):
        line(b, B, 1, dist, lambda t, slot, to, *rest: ycopy(slot, to).wait_send())
        for h in range(len(spans)):
            for s in range(A):
                def left(t, slot, to, *rest, h=h, d=pick(s)):
                    inner_copy(h, d, slot, to).wait_send()

                line(b, B, 1, dist, left)
    for h in range(len(spans)):
        for s in range(A - 1):
            outer_copy(h, s)[-1].wait_send()


def sorted_table(count):
    return [sorted(range(count), key=lambda d: (-abs(d - i), -d)) for i in range(count)]


def body(vectors, tile_values, tile_rows, tile_cols, tile_count, degrees):
    R = lax.axis_size("row")
    C = lax.axis_size("col")
    piece, width = vectors.shape
    side = tile_values.shape[-1]
    slots = tile_values.shape[2]
    B = inner_size(C)
    A = C // B
    tpp = piece // side
    chips = R // 2
    dims = (R, A, B, piece, width, side, slots)
    vmem = pl.BlockSpec(memory_space=pltpu.VMEM)
    smem = pl.BlockSpec(memory_space=pltpu.SMEM)
    dma = pltpu.SemaphoreType.DMA
    f32 = jnp.float32
    far = max(chips - 1, 1)
    tail_rows = -(-piece // 96) * 16
    return pl.pallas_call(
        functools.partial(kernel, dims),
        out_shape=jax.ShapeDtypeStruct((piece, width), f32),
        in_specs=[smem, smem, smem, pl.BlockSpec(memory_space=pl.ANY), vmem, pl.BlockSpec(memory_space=pl.ANY)],
        out_specs=vmem,
        scratch_shapes=[
            pltpu.VMEM((slots, side, side), tile_values.dtype),
            pltpu.VMEM((R, piece, width), f32),
            pltpu.VMEM((R * tpp, side, 2 * width), jnp.bfloat16),
            pltpu.VMEM((slots + 1, side, width), f32),
            pltpu.VMEM((A, B + 1, piece - tail_rows, width), f32),
            pltpu.VMEM((A + 1, piece - tail_rows, width), f32),
            pltpu.VMEM((A + 1, B, tail_rows, width), f32),
            pltpu.VMEM((B + 1, tail_rows, width), f32),
            pltpu.SMEM((slots,), jnp.int32),
            pltpu.SMEM((C * tpp,), jnp.int32),
            dma, dma,
            dma((far, tpp)), dma((far, tpp)),
            dma((tpp,)), dma((tpp,)),
            dma((far, tpp)), dma((far, tpp)),
            dma((2, A, B + 1)), dma((2, A, B + 1)),
            dma((2, A + 1)), dma((2, A + 1)),
            dma((A + 1,)), dma((A + 1,)),
            dma((B + 1,)), dma((B + 1,)),
        ],
        compiler_params=pltpu.CompilerParams(
            collective_id=0, has_side_effects=True, vmem_limit_bytes=67043328
        ),
    )(tile_rows, tile_cols, tile_count, vectors, degrees.reshape(-1, 128), tile_values)


def solution(mesh):
    placed = (
        P(("col", "row"), None),
        P("row", "col", None, None, None),
        P("row", "col", None),
        P("row", "col", None),
        P("row", "col"),
        P(),
    )
    return jax.shard_map(
        body, mesh=mesh, in_specs=placed, out_specs=P(("row", "col"), None), check_vma=False
    )
```

profile of v0, /device:TPU:0, one launch (start us, length us, event | category | flops | bytes accessed | tf_op | source)
XLA Modules:
  0.0 70.7 jit_solution(18028429950329175754)
XLA Ops:
  0.7 68.1 %shard_map.64 = f32[1024,128]{1,0:T(8,128)} custom-call(s32[1,1,22]{2,1,0:T(1,128)} %rows_s.1, s32[1,1,22]{2,1,0:T(1,128)} %cols_s.1, s32[1,1]{1,0:T(1,128)S(6)} %copy.8.count_s, f32[1024,128]{1,0:T(8,128)} %vec_ref.1, s32[256,128]{1,0:T(8,128)} %bitcast.1, bf16[1,1,22,512,512]{4,3,2,1,0:T(8,128)(2,1)} %tiles_hbm.1), custom_call_target="tpu_custom_call" | custom-call | tf_op jit(solution)/shard_map/pallas_call | solution.py:411
  68.8 1.9 %copy.9 = f32[1024,128]{1,0:T(8,128)} copy(f32[1024,128]{1,0:T(8,128)} %shard_map.64) | data formatting | bytes 1048576
where the time goes:
time: 70.8 us; the launch traced here: 70.7 us
  Pallas kernels  68.1 us (96%)
  local copies, waits for them, and re-layouts  1.87 us (3%)
    pallas_call x1, Pallas kernels, body(): pl.pallas_call(functools.partial(kernel, dims), out_shape=jax.ShapeDtypeS...  68.1 us
    unnamed x1, local copies, waits for them, and re-layouts  1.87 us

commit v1 on v0

v1 whole, which is shorter than its diff:
```python
import functools

import jax
import jax.numpy as jnp
from jax import lax
from jax.experimental import pallas as pl
from jax.experimental.pallas import tpu as pltpu
from jax.sharding import PartitionSpec as P

MESH = pl.DeviceIdType.MESH
LANES = 128
SLICES = 4
CHUNK = 32


def inner_size(col_count):
    inner = 1
    while inner * inner * 4 <= col_count and col_count % (inner * 2) == 0:
        inner *= 2
    return inner


def sorted_table(count):
    return [sorted(range(count), key=lambda d: (-abs(d - i), -d)) for i in range(count)]


def tail_rows(packed):
    return (packed // 2, packed // 4) + (0,) * (SLICES - 2)


def kernel(
    dims,
    rows_s, cols_s, count_s, vec_hbm, deg_hbm, tiles_hbm, out_ref,
    tiles_v, vec_v, deg_v, fin, fout, gath, rhs, sums, part, inb, outb, zb, yb, prev_s, last_s,
    tile_sem, vec_sem, deg_sem, d_send, d_recv, m_send, m_recv, f_send, f_recv,
    i_send, i_recv, o_send, o_recv, z_send, z_recv, y_send, y_recv,
):
    R, A, B, piece, width, side, slots = dims
    C = A * B
    S = SLICES
    gw = width // S
    packed = piece // S
    tpp = piece // side
    halves = S // tpp
    blocks = packed // LANES
    tails = tail_rows(packed)
    tailed = [s for s in range(S) if tails[s]]
    chips = R // 2
    me_row = lax.axis_index("row")
    me_col = lax.axis_index("col")
    chip, core = me_row // 2, me_row % 2
    mate = chip * 2 + (1 - core)
    a, b = me_col // B, me_col % B
    f32 = jnp.float32

    def rdma(src, dst, ssem, rsem, where):
        return pltpu.make_async_remote_copy(
            src_ref=src, dst_ref=dst, send_sem=ssem, recv_sem=rsem,
            device_id=where, device_id_type=MESH,
        )

    vec_copy = pltpu.make_async_copy(vec_hbm, vec_v, vec_sem)
    vec_copy.start()
    deg_n = piece // LANES
    deg_at = (me_col * R + me_row, me_row * C + me_col)
    deg_copies = []
    for i, at in enumerate(deg_at):
        cp = pltpu.make_async_copy(
            deg_hbm.at[pl.ds(pl.multiple_of(at * deg_n, deg_n), deg_n)], deg_v.at[i], deg_sem.at[i])
        cp.start()
        deg_copies.append(cp)
    tile_copy = pltpu.make_async_copy(tiles_hbm.at[0, 0], tiles_v, tile_sem)
    tile_copy.start()

    barrier = pltpu.get_barrier_semaphore()

    def greet(where):
        pl.semaphore_signal(barrier, inc=1, device_id=where, device_id_type=MESH)

    greet({"row": mate})
    for j in range(1, chips):
        greet({"row": lax.rem(chip + j, chips) * 2 + core})
    conds = []
    if B > 1:
        conds += [(b > 0, me_col - 1), (b < B - 1, me_col + 1)]
    if A > 1:
        conds += [(a > 0, me_col - B), (a < A - 1, me_col + B)]
    for cond, other in conds:
        @pl.when(cond)
        def _(other=other):
            greet({"col": other})
    peers = jnp.int32(chips)
    for cond, other in conds:
        peers = peers + jnp.where(cond, 1, 0)

    group = lax.broadcasted_iota(jnp.int32, (CHUNK, LANES), 1) // gw
    odd = group % 2 == 1

    def place(q):
        u, h = q // halves, q % halves
        return u, h

    def first_row(blk, h):
        return (blk * halves + h) * LANES

    def by_group(values):
        out = values[S - 1]
        for g in range(S - 2, -1, -1):
            out = jnp.where(group == g, values[g], out)
        return out

    def roll(x, steps):
        steps = steps % S
        return pltpu.roll(x, steps * gw, 1) if steps else x

    for cp in deg_copies:
        cp.wait()
    for i, ref in enumerate((fin, fout)):
        f = lax.rsqrt(deg_v[i].astype(f32))
        for blk in range(blocks):
            rows = []
            for q in range(S):
                u, h = place(q)
                at = u * (side // LANES) + blk * halves + h
                rows.append(jnp.broadcast_to(f[at:at + 1, :], (gw, LANES)))
            ref[blk * LANES:(blk + 1) * LANES, :] = jnp.concatenate(rows, 0).T

    vec_copy.wait()
    for blk in range(blocks):
        def pack_own(c, _, blk=blk):
            at = pl.multiple_of(c * CHUNK, CHUNK)
            v = []
            for q in range(S):
                u, h = place(q)
                v.append(vec_v[pl.ds(u * side + first_row(blk, h) + at, CHUNK)])
            to = pl.ds(blk * LANES + at, CHUNK)
            f = fin[to]
            for s in range(S):
                x = by_group([roll(v[q], q - s) for q in range(S)])
                gath[s, me_row, to] = x * f
            return 0

        lax.fori_loop(0, LANES // CHUNK, pack_own, 0)

    pl.semaphore_wait(barrier, peers)

    directs, mates, forwards = {}, {}, {}
    for s in range(S):
        for j in range(1, chips):
            dst = lax.rem(chip + j, chips) * 2 + core
            cp = rdma(gath.at[s, me_row], gath.at[s, me_row],
                      d_send.at[j - 1, s], d_recv.at[j - 1, s], {"row": dst})
            cp.start()
            directs[j, s] = cp
        cp = rdma(gath.at[s, me_row], gath.at[s, me_row],
                  m_send.at[s], m_recv.at[s], {"row": mate})
        cp.start()
        mates[s] = cp

    count = count_s[0, 0]

    def link(k, _):
        rk = rows_s[0, 0, k]
        v = jnp.int32(slots)
        for j in range(slots):
            v = jnp.where((rows_s[0, 0, j] == rk) & (j < k), j, v)
        prev_s[k] = v
        return 0

    def ends(r, _):
        v = jnp.int32(slots)
        for j in range(slots):
            v = jnp.where((rows_s[0, 0, j] == r) & (j < count), j, v)
        last_s[r] = v
        return 0

    def landed(s, r, ssem, rsem):
        rdma(gath.at[s, r], gath.at[s, r], ssem, rsem, {"row": mate}).wait_recv()

    def operand(s, r):
        for blk in range(blocks):
            def step(c, _, blk=blk):
                at = pl.multiple_of(c * CHUNK, CHUNK)
                x = gath[s, r, pl.ds(blk * LANES + at, CHUNK)]
                turned = [roll(x, n) for n in range(S)]
                for q in range(S):
                    u, h = place(q)
                    rep = by_group([turned[(g - q) % S] for g in range(S)])
                    hi = rep.astype(jnp.bfloat16).astype(f32)
                    v = jnp.where(odd, rep - hi, hi)
                    rhs[r * tpp + u, pl.ds(first_row(blk, h) + at, CHUNK), :] = v.astype(jnp.bfloat16)
                return 0

            lax.fori_loop(0, LANES // CHUNK, step, 0)

    def forward(s):
        for j in range(1, chips):
            src = lax.rem(chip - j + chips, chips) * 2 + core
            landed(s, src, d_send.at[j - 1, s], d_recv.at[j - 1, s])
            cp = rdma(gath.at[s, src], gath.at[s, src],
                      f_send.at[j - 1, s], f_recv.at[j - 1, s], {"row": mate})
            cp.start()
            forwards[j, s] = cp

    def operands_own(s):
        operand(s, me_row)
        landed(s, mate, m_send.at[s], m_recv.at[s])
        operand(s, mate)

    def operands_far(s):
        for j in range(1, chips):
            operand(s, lax.rem(chip - j + chips, chips) * 2 + core)
        for j in range(1, chips):
            src = lax.rem(chip - j + chips, chips) * 2 + (1 - core)
            landed(s, src, f_send.at[j - 1, s], f_recv.at[j - 1, s])
            operand(s, src)

    def products(lo, n):
        def product(k, _):
            both = jnp.dot(tiles_v[k, lo:lo + n], rhs[cols_s[0, 0, k]],
                           preferred_element_type=f32)
            sums[k, lo:lo + n] = both + sums[prev_s[k], lo:lo + n]
            return 0

        lax.fori_loop(0, slots, product, 0, unroll=True)

    def pack(s, blk):
        def step(dest, _):
            for c in range(0, LANES, CHUNK):
                v = []
                for q in range(S):
                    u, h = place(q)
                    at = first_row(blk, h) + c
                    v.append(sums[last_s[dest * tpp + u], at:at + CHUNK])
                x = by_group(v)
                y = by_group([v[(g + 1) % S] for g in range(S)])
                at = blk * LANES + c
                part[s, dest, at:at + CHUNK] = x + roll(y, 1)
            return 0

        lax.fori_loop(0, C, step, 0)

    order = sorted_table(A)

    def pick(i):
        v = jnp.int32(order[0][i])
        for n in range(1, A):
            v = jnp.where(a == n, order[n][i], v)
        return v

    def line(pos, size, stride, dist, action):
        for right in (True, False):
            t = pos + dist if right else pos - dist
            slot = t + 1 if right else t
            to = me_col + stride if right else me_col - stride
            more = pos > 0 if right else pos < size - 1

            @pl.when((t < size) if right else (t >= 0))
            def _(t=t, slot=slot, to=to, more=more):
                action(t, slot, to, more, dist < size - 1)

    def arrive(pos, size, ref, ssem, rsem, fold):
        if size > 1:
            for cond, slot in ((pos > 0, pos + 1), (pos < size - 1, pos)):
                @pl.when(cond)
                def _(slot=slot):
                    rdma(ref(slot), ref(slot), ssem(slot), rsem(slot), {"row": mate}).wait_recv()
        if size > 2:
            @pl.when((pos > 0) & (pos < size - 1))
            def _():
                fold(pos + 1, pos)

    near = jnp.where(b > 0, b + 1, 0)
    near_a = jnp.where(a > 0, a + 1, 0)

    def rest(s):
        return pl.ds(tails[s], packed - tails[s])

    def inner_copy(s, d, t, slot, to):
        return rdma(part.at[s, d * B + t, rest(s)], inb.at[s, d, slot, rest(s)],
                    i_send.at[s, d, slot], i_recv.at[s, d, slot], {"col": to})

    def inner_send(s, i):
        d = pick(i)

        def action(t, slot, to, more, can):
            cp = inner_copy(s, d, t, slot, to)
            if can:
                @pl.when(more)
                def _():
                    cp.wait_recv()
                    at = rest(s)
                    part[s, d * B + t, at] = part[s, d * B + t, at] + inb[s, d, slot, at]
            cp.start()

        for dist in range(B - 1, 0, -1):
            line(b, B, 1, dist, action)

    def inner_done(s, d):
        at = rest(s)

        def fold(x, y):
            inb[s, d, x, at] = inb[s, d, x, at] + inb[s, d, y, at]

        arrive(b, B, lambda q: inb.at[s, d, q, at], lambda q: i_send.at[s, d, q],
               lambda q: i_recv.at[s, d, q], fold)

    def here(s, d, at):
        v = part[s, d * B + b, at]
        if B > 1:
            v = v + inb[s, d, near, at]
        return v

    def outer_copy(s, i):
        d = pick(i)
        right = d > a
        slot = jnp.where(right, d + 1, d)
        to = jnp.where(right, me_col + B, me_col - B)
        more = (right & (a > 0)) | (jnp.logical_not(right) & (a < A - 1))
        cp = rdma(part.at[s, d * B + b, rest(s)], outb.at[s, slot, rest(s)],
                  o_send.at[s, slot], o_recv.at[s, slot], {"col": to})
        return d, slot, more, cp

    def outer_step(s, i, now):
        d, slot, more, cp = outer_copy(s, i)
        at = rest(s)
        if now:
            @pl.when(jnp.logical_not(more))
            def _():
                inner_done(s, d)
                part[s, d * B + b, at] = here(s, d, at)
                cp.start()
        else:
            @pl.when(more)
            def _():
                inner_done(s, d)
                cp.wait_recv()
                part[s, d * B + b, at] = here(s, d, at) + outb[s, slot, at]
                cp.start()

    def tail_copy(s, d, slot, to):
        rows = pl.ds(0, tails[s])
        return rdma(part.at[s, pl.ds(d * B, B), rows], zb.at[s, slot, :, rows],
                    z_send.at[s, slot], z_recv.at[s, slot], {"col": to})

    def tail_send(s, dist, now):
        rows = pl.ds(0, tails[s])

        def action(d, slot, to, more, can):
            cp = tail_copy(s, d, slot, to)
            if now:
                @pl.when(jnp.logical_not(more))
                def _():
                    cp.start()
            elif can:
                @pl.when(more)
                def _():
                    cp.wait_recv()
                    for t in range(B):
                        part[s, d * B + t, rows] = part[s, d * B + t, rows] + zb[s, slot, t, rows]
                    cp.start()

        line(a, A, B, dist, action)

    def turn_copy(s, t, slot, to):
        rows = pl.ds(0, tails[s])
        return rdma(part.at[s, a * B + t, rows], yb.at[s, slot, rows],
                    y_send.at[s, slot], y_recv.at[s, slot], {"col": to})

    def turn(s):
        rows = pl.ds(0, tails[s])

        def fold(x, y):
            zb[s, x, :, rows] = zb[s, x, :, rows] + zb[s, y, :, rows]

        arrive(a, A, lambda q: zb.at[s, q, :, rows], lambda q: z_send.at[s, q],
               lambda q: z_recv.at[s, q], fold)

        def action(t, slot, to, more, can):
            cp = turn_copy(s, t, slot, to)
            v = part[s, a * B + t, rows]
            if A > 1:
                v = v + zb[s, near_a, t, rows]
            part[s, a * B + t, rows] = v
            if can:
                @pl.when(more)
                def _():
                    cp.wait_recv()
                    part[s, a * B + t, rows] = part[s, a * B + t, rows] + yb[s, slot, rows]
            cp.start()

        for dist in range(B - 1, 0, -1):
            line(b, B, 1, dist, action)

    def write(s, lo, hi, get):
        for at in range(lo, hi, CHUNK):
            blk, c = at // LANES, at % LANES
            total = get(pl.ds(at, CHUNK)) * fout[at:at + CHUNK]
            for q in range(S):
                u, h = place(q)
                to = u * side + first_row(blk, h) + c
                out_ref[to:to + CHUNK, s * gw:(s + 1) * gw] = roll(total, s - q)[:, s * gw:(s + 1) * gw]

    def finish(s):
        at = rest(s)
        inner_done(s, a)
        if A > 1:
            def fold(x, y):
                outb[s, x, at] = outb[s, x, at] + outb[s, y, at]

            arrive(a, A, lambda q: outb.at[s, q, at], lambda q: o_send.at[s, q],
                   lambda q: o_recv.at[s, q], fold)

        def get(rows):
            v = here(s, a, rows)
            if A > 1:
                v = v + outb[s, near_a, rows]
            return v

        write(s, tails[s], packed, get)

    def finish_tail(s):
        rows = pl.ds(0, tails[s])

        def fold(x, y):
            yb[s, x, rows] = yb[s, x, rows] + yb[s, y, rows]

        arrive(b, B, lambda q: yb.at[s, q, rows], lambda q: y_send.at[s, q],
               lambda q: y_recv.at[s, q], fold)

        def get(rows):
            v = part[s, a * B + b, rows]
            if A > 1:
                v = v + zb[s, near_a, b, rows]
            if B > 1:
                v = v + yb[s, near, rows]
            return v

        write(s, 0, tails[s], get)

    lax.fori_loop(0, slots, link, 0)
    lax.fori_loop(0, C * tpp, ends, 0)
    sums[slots] = jnp.zeros((side, LANES), f32)

    def all_tails(s, now, dists):
        if A > 1:
            for dist in dists:
                tail_send(s, dist, now)

    every = range(A - 1, 0, -1)

    operands_own(0)
    forward(0)
    operands_far(0)
    tile_copy.wait()
    span = side // blocks
    for blk in range(blocks):
        products(blk * span, span)
        pack(0, blk)
        if blk == 0:
            all_tails(0, True, every)
            forward(1)
    for i in range(A):
        inner_send(0, i)
    forward(2)
    operands_own(1)
    operands_far(1)
    products(0, side)
    for blk in range(blocks):
        pack(1, blk)
    all_tails(1, True, every)
    for i in range(A):
        inner_send(1, i)
    all_tails(0, False, list(every)[:-1])
    forward(3)
    operands_own(2)
    operands_far(2)
    products(0, side)
    for blk in range(blocks):
        pack(2, blk)
    inner_send(2, 0)
    for i in range(A - 1):
        outer_step(0, i, True)
    all_tails(0, False, list(every)[-1:])
    operands_own(3)
    operands_far(3)
    products(0, side)
    for blk in range(blocks):
        pack(3, blk)
    inner_send(3, 0)
    for i in range(1, A):
        inner_send(2, i)
        inner_send(3, i)
    all_tails(1, False, every)
    for s in (0, 1):
        for i in range(A - 1):
            if s > 0:
                outer_step(s, i, True)
            outer_step(s, i, False)
    turn(0)
    turn(1)
    for i in range(A - 1):
        for s in (2, 3):
            outer_step(s, i, True)
            outer_step(s, i, False)
        if i < 2:
            finish(i)
    for s in range(min(2, A - 1), S):
        finish(s)
    for s in tailed:
        finish_tail(s)

    for sent in (directs.values(), mates.values(), forwards.values()):
        for cp in sent:
            cp.wait_send()
    for s in tailed:
        for dist in every:
            line(a, A, B, dist, lambda d, slot, to, *rest, s=s: tail_copy(s, d, slot, to).wait_send())
        for dist in range(B - 1, 0, -1):
            line(b, B, 1, dist, lambda t, slot, to, *rest, s=s: turn_copy(s, t, slot, to).wait_send())
    for s in range(S):
        for i in range(A):
            for dist in range(B - 1, 0, -1):
                def left(t, slot, to, *rest, s=s, d=pick(i)):
                    inner_copy(s, d, t, slot, to).wait_send()

                line(b, B, 1, dist, left)
        for i in range(A - 1):
            outer_copy(s, i)[-1].wait_send()


def body(vectors, tile_values, tile_rows, tile_cols, tile_count, degrees):
    R = lax.axis_size("row")
    C = lax.axis_size("col")
    piece, width = vectors.shape
    side = tile_values.shape[-1]
    slots = tile_values.shape[2]
    B = inner_size(C)
    A = C // B
    tpp = piece // side
    chips = R // 2
    dims = (R, A, B, piece, width, side, slots)
    vmem = pl.BlockSpec(memory_space=pltpu.VMEM)
    smem = pl.BlockSpec(memory_space=pltpu.SMEM)
    anywhere = pl.BlockSpec(memory_space=pl.ANY)
    dma = pltpu.SemaphoreType.DMA
    f32 = jnp.float32
    far = max(chips - 1, 1)
    S = SLICES
    packed = piece // S
    tails = tail_rows(packed)
    kinds = sum(1 for n in tails if n)
    return pl.pallas_call(
        functools.partial(kernel, dims),
        out_shape=jax.ShapeDtypeStruct((piece, width), f32),
        in_specs=[smem, smem, smem, anywhere, anywhere, anywhere],
        out_specs=vmem,
        scratch_shapes=[
            pltpu.VMEM((slots, side, side), tile_values.dtype),
            pltpu.VMEM((piece, width), f32),
            pltpu.VMEM((2, piece // LANES, LANES), jnp.int32),
            pltpu.VMEM((packed, LANES), f32),
            pltpu.VMEM((packed, LANES), f32),
            pltpu.VMEM((S, R, packed, LANES), f32),
            pltpu.VMEM((R * tpp, side, LANES), jnp.bfloat16),
            pltpu.VMEM((slots + 1, side, LANES), f32),
            pltpu.VMEM((S, C, packed, LANES), f32),
            pltpu.VMEM((S, A, B + 1, packed, LANES), f32),
            pltpu.VMEM((S, A + 1, packed, LANES), f32),
            pltpu.VMEM((kinds, A + 1, B, max(tails), LANES), f32),
            pltpu.VMEM((kinds, B + 1, max(tails), LANES), f32),
            pltpu.SMEM((slots,), jnp.int32),
            pltpu.SMEM((C * tpp,), jnp.int32),
            dma, dma, dma((2,)),
            dma((far, S)), dma((far, S)),
            dma((S,)), dma((S,)),
            dma((far, S)), dma((far, S)),
            dma((S, A, B + 1)), dma((S, A, B + 1)),
            dma((S, A + 1)), dma((S, A + 1)),
            dma((kinds, A + 1)), dma((kinds, A + 1)),
            dma((kinds, B + 1)), dma((kinds, B + 1)),
        ],
        compiler_params=pltpu.CompilerParams(
            collective_id=0, has_side_effects=True, vmem_limit_bytes=67043328
        ),
    )(tile_rows, tile_cols, tile_count, vectors, degrees.reshape(-1, LANES), tile_values)


def solution(mesh):
    placed = (
        P(("col", "row"), None),
        P("row", "col", None, None, None),
        P("row", "col", None),
        P("row", "col", None),
        P("row", "col"),
        P(),
    )
    return jax.shard_map(
        body, mesh=mesh, in_specs=placed, out_specs=P(("row", "col"), None), check_vma=False
    )
```

time: 70.8 us -> 73.8 us (1.042)
  Pallas kernels: 68.1 us -> 71.1 us
    pallas_call x1, Pallas kernels: 68.1 us -> 71.1 us  [body(): pl.pallas_call(functools.partial(kernel, dims), out_shape=jax.ShapeDtypeS...]
where the time goes in v1:
time: 73.8 us; the launch traced here: 73.6 us
  Pallas kernels  71.1 us (96%)
  local copies, waits for them, and re-layouts  1.87 us (3%)
    pallas_call x1, Pallas kernels, body(): pl.pallas_call(functools.partial(kernel, dims), out_shape=jax.ShapeDtypeS...  71.1 us
    unnamed x1, local copies, waits for them, and re-layouts  1.87 us

profile of v1, /device:TPU:0, one launch (start us, length us, event | category | flops | bytes accessed | tf_op | source)
XLA Modules:
  0.0 73.6 jit_solution(16241756407163719014)
XLA Ops:
  0.7 71.1 %shard_map.64 = f32[1024,128]{1,0:T(8,128)} custom-call(s32[1,1,22]{2,1,0:T(1,128)} %rows_s.1, s32[1,1,22]{2,1,0:T(1,128)} %cols_s.1, s32[1,1]{1,0:T(1,128)S(6)} %copy.8.count_s, f32[1024,128]{1,0:T(8,128)} %vec_hbm.1, s32[256,128]{1,0:T(8,128)} %bitcast.1, bf16[1,1,22,512,512]{4,3,2,1,0:T(8,128)(2,1)} %tiles_hbm.1), custom_call_target="tpu_custom_call" | custom-call | tf_op jit(solution)/shard_map/pallas_call | solution.py:553
  71.8 1.9 %copy.9 = f32[1024,128]{1,0:T(8,128)} copy(f32[1024,128]{1,0:T(8,128)} %shard_map.64) | data formatting | bytes 1048576

commit v2 on v1

--- a/solution.py
+++ b/solution.py
@@ -125,27 +125,20 @@
                 rows.append(jnp.broadcast_to(f[at:at + 1, :], (gw, LANES)))
             ref[blk * LANES:(blk + 1) * LANES, :] = jnp.concatenate(rows, 0).T
 
-    vec_copy.wait()
-    for blk in range(blocks):
-        def pack_own(c, _, blk=blk):
-            at = pl.multiple_of(c * CHUNK, CHUNK)
-            v = []
-            for q in range(S):
-                u, h = place(q)
-                v.append(vec_v[pl.ds(u * side + first_row(blk, h) + at, CHUNK)])
-            to = pl.ds(blk * LANES + at, CHUNK)
-            f = fin[to]
-            for s in range(S):
-                x = by_group([roll(v[q], q - s) for q in range(S)])
-                gath[s, me_row, to] = x * f
-            return 0
-
-        lax.fori_loop(0, LANES // CHUNK, pack_own, 0)
-
-    pl.semaphore_wait(barrier, peers)
+    def pack_own(s):
+        for blk in range(blocks):
+            for c in range(0, LANES, CHUNK):
+                v = []
+                for q in range(S):
+                    u, h = place(q)
+                    at = u * side + first_row(blk, h) + c
+                    v.append(roll(vec_v[at:at + CHUNK], q - s))
+                to = blk * LANES + c
+                gath[s, me_row, to:to + CHUNK] = by_group(v) * fin[to:to + CHUNK]
 
     directs, mates, forwards = {}, {}, {}
-    for s in range(S):
+
+    def send_own(s):
         for j in range(1, chips):
             dst = lax.rem(chip + j, chips) * 2 + core
             cp = rdma(gath.at[s, me_row], gath.at[s, me_row],
@@ -157,6 +150,14 @@
         cp.start()
         mates[s] = cp
 
+    vec_copy.wait()
+    pack_own(0)
+    pl.semaphore_wait(barrier, peers)
+    send_own(0)
+    for s in range(1, S):
+        pack_own(s)
+        send_own(s)
+
     count = count_s[0, 0]
 
     def link(k, _):
@@ -177,21 +178,25 @@
     def landed(s, r, ssem, rsem):
         rdma(gath.at[s, r], gath.at[s, r], ssem, rsem, {"row": mate}).wait_recv()
 
-    def operand(s, r):
+    low = group < S // 2
+
+    def operand(s, r, lane):
         for blk in range(blocks):
-            def step(c, _, blk=blk):
-                at = pl.multiple_of(c * CHUNK, CHUNK)
-                x = gath[s, r, pl.ds(blk * LANES + at, CHUNK)]
-                turned = [roll(x, n) for n in range(S)]
+            for c in range(0, LANES, CHUNK):
+                at = blk * LANES + c
+                x = gath[s, r, at:at + CHUNK]
+                hi = x.astype(jnp.bfloat16).astype(f32)
+                lo = x - hi
+                same, swapped = jnp.where(odd, lo, hi), jnp.where(odd, hi, lo)
+                t = (same, roll(swapped, 1), roll(same, 2), roll(swapped, 3))
+                e, f = jnp.where(odd, t[1], t[0]), jnp.where(odd, t[3], t[2])
+                g, k = jnp.where(odd, t[0], t[3]), jnp.where(odd, t[2], t[1])
+                spread = (jnp.where(low, e, f), jnp.where(low, g, k),
+                          jnp.where(low, f, e), jnp.where(low, k, g))
                 for q in range(S):
                     u, h = place(q)
-                    rep = by_group([turned[(g - q) % S] for g in range(S)])
-                    hi = rep.astype(jnp.bfloat16).astype(f32)
-                    v = jnp.where(odd, rep - hi, hi)
-                    rhs[r * tpp + u, pl.ds(first_row(blk, h) + at, CHUNK), :] = v.astype(jnp.bfloat16)
-                return 0
-
-            lax.fori_loop(0, LANES // CHUNK, step, 0)
+                    to = first_row(blk, h) + c
+                    rhs[r * tpp + u, to:to + CHUNK, lane:lane + LANES] = spread[q].astype(jnp.bfloat16)
 
     def forward(s):
         for j in range(1, chips):
@@ -202,43 +207,45 @@
             cp.start()
             forwards[j, s] = cp
 
-    def operands_own(s):
-        operand(s, me_row)
+    def arrivals(s):
         landed(s, mate, m_send.at[s], m_recv.at[s])
-        operand(s, mate)
-
-    def operands_far(s):
-        for j in range(1, chips):
-            operand(s, lax.rem(chip - j + chips, chips) * 2 + core)
         for j in range(1, chips):
             src = lax.rem(chip - j + chips, chips) * 2 + (1 - core)
             landed(s, src, f_send.at[j - 1, s], f_recv.at[j - 1, s])
-            operand(s, src)
-
-    def products(lo, n):
+
+    def operands(s, lane):
+        def step(r, _):
+            operand(s, r, lane)
+            return 0
+
+        lax.fori_loop(0, R, step, 0)
+
+    span = side // blocks
+
+    def products(blk, lanes):
         def product(k, _):
-            both = jnp.dot(tiles_v[k, lo:lo + n], rhs[cols_s[0, 0, k]],
+            both = jnp.dot(tiles_v[k, blk * span:(blk + 1) * span], rhs[cols_s[0, 0, k], :, :lanes],
                            preferred_element_type=f32)
-            sums[k, lo:lo + n] = both + sums[prev_s[k], lo:lo + n]
+            sums[k, :, :lanes] = both + sums[prev_s[k], :, :lanes]
             return 0
 
         lax.fori_loop(0, slots, product, 0, unroll=True)
 
-    def pack(s, blk):
+    def pack(s, blk, lane):
         def step(dest, _):
             for c in range(0, LANES, CHUNK):
                 v = []
                 for q in range(S):
                     u, h = place(q)
-                    at = first_row(blk, h) + c
-                    v.append(sums[last_s[dest * tpp + u], at:at + CHUNK])
+                    at = h * LANES + c
+                    v.append(sums[last_s[dest * tpp + u], at:at + CHUNK, lane:lane + LANES])
                 x = by_group(v)
                 y = by_group([v[(g + 1) % S] for g in range(S)])
                 at = blk * LANES + c
                 part[s, dest, at:at + CHUNK] = x + roll(y, 1)
             return 0
 
-        lax.fori_loop(0, C, step, 0)
+        lax.fori_loop(0, C, step, 0, unroll=4)
 
     order = sorted_table(A)
 
@@ -440,7 +447,7 @@
 
     lax.fori_loop(0, slots, link, 0)
     lax.fori_loop(0, C * tpp, ends, 0)
-    sums[slots] = jnp.zeros((side, LANES), f32)
+    sums[slots] = jnp.zeros((span, 2 * LANES), f32)
 
     def all_tails(s, now, dists):
         if A > 1:
@@ -449,46 +456,49 @@
 
     every = range(A - 1, 0, -1)
 
-    operands_own(0)
+    operand(0, me_row, 0)
+    landed(0, mate, m_send.at[0], m_recv.at[0])
+    operand(0, mate, 0)
     forward(0)
-    operands_far(0)
+    for j in range(1, chips):
+        operand(0, lax.rem(chip - j + chips, chips) * 2 + core, 0)
+    for j in range(1, chips):
+        src = lax.rem(chip - j + chips, chips) * 2 + (1 - core)
+        landed(0, src, f_send.at[j - 1, 0], f_recv.at[j - 1, 0])
+        operand(0, src, 0)
     tile_copy.wait()
-    span = side // blocks
     for blk in range(blocks):
-        products(blk * span, span)
-        pack(0, blk)
+        products(blk, LANES)
+        pack(0, blk, 0)
         if blk == 0:
             all_tails(0, True, every)
             forward(1)
     for i in range(A):
         inner_send(0, i)
     forward(2)
-    operands_own(1)
-    operands_far(1)
-    products(0, side)
+    arrivals(1)
+    operands(1, 0)
     for blk in range(blocks):
-        pack(1, blk)
-    all_tails(1, True, every)
+        products(blk, LANES)
+        pack(1, blk, 0)
+        if blk == 0:
+            all_tails(1, True, every)
     for i in range(A):
         inner_send(1, i)
+    forward(3)
     all_tails(0, False, list(every)[:-1])
-    forward(3)
-    operands_own(2)
-    operands_far(2)
-    products(0, side)
+    for s in (2, 3):
+        arrivals(s)
+        operands(s, (s - 2) * LANES)
     for blk in range(blocks):
-        pack(2, blk)
-    inner_send(2, 0)
-    for i in range(A - 1):
-        outer_step(0, i, True)
-    all_tails(0, False, list(every)[-1:])
-    operands_own(3)
-    operands_far(3)
-    products(0, side)
-    for blk in range(blocks):
-        pack(3, blk)
-    inner_send(3, 0)
-    for i in range(1, A):
+        products(blk, 2 * LANES)
+        for s in (2, 3):
+            pack(s, blk, (s - 2) * LANES)
+        if blk == 0:
+            for i in range(A - 1):
+                outer_step(0, i, True)
+            all_tails(0, False, list(every)[-1:])
+    for i in range(A):
         inner_send(2, i)
         inner_send(3, i)
     all_tails(1, False, every)
@@ -562,8 +572,8 @@
             pltpu.VMEM((packed, LANES), f32),
             pltpu.VMEM((packed, LANES), f32),
             pltpu.VMEM((S, R, packed, LANES), f32),
-            pltpu.VMEM((R * tpp, side, LANES), jnp.bfloat16),
-            pltpu.VMEM((slots + 1, side, LANES), f32),
+            pltpu.VMEM((R * tpp, side, 2 * LANES), jnp.bfloat16),
+            pltpu.VMEM((slots + 1, side * LANES * S // piece, 2 * LANES), f32),
             pltpu.VMEM((S, C, packed, LANES), f32),
             pltpu.VMEM((S, A, B + 1, packed, LANES), f32),
             pltpu.VMEM((S, A + 1, packed, LANES), f32),

time: 73.8 us -> 62.7 us (0.85)
  Pallas kernels: 71.1 us -> 60 us
    pallas_call x1, Pallas kernels: 71.1 us -> 60 us  [body(): pl.pallas_call(functools.partial(kernel, dims), out_shape=jax.ShapeDtypeS...]
where the time goes in v2:
time: 62.7 us; the launch traced here: 62.5 us
  Pallas kernels  60 us (96%)
  local copies, waits for them, and re-layouts  1.87 us (3%)
  between operations  0.66 us (1%)
    pallas_call x1, Pallas kernels, body(): pl.pallas_call(functools.partial(kernel, dims), out_shape=jax.ShapeDtypeS...  60 us
    unnamed x1, local copies, waits for them, and re-layouts  1.87 us

profile of v2, /device:TPU:0, one launch (start us, length us, event | category | flops | bytes accessed | tf_op | source)
XLA Modules:
  0.0 62.5 jit_solution(13817418932072389155)
XLA Ops:
  0.7 60.0 %shard_map.64 = f32[1024,128]{1,0:T(8,128)} custom-call(s32[1,1,22]{2,1,0:T(1,128)} %rows_s.1, s32[1,1,22]{2,1,0:T(1,128)} %cols_s.1, s32[1,1]{1,0:T(1,128)S(6)} %copy.8.count_s, f32[1024,128]{1,0:T(8,128)} %vec_hbm.1, s32[256,128]{1,0:T(8,128)} %bitcast.1, bf16[1,1,22,512,512]{4,3,2,1,0:T(8,128)(2,1)} %tiles_hbm.1), custom_call_target="tpu_custom_call" | custom-call | tf_op jit(solution)/shard_map/pallas_call | solution.py:563
  60.6 1.9 %copy.9 = f32[1024,128]{1,0:T(8,128)} copy(f32[1024,128]{1,0:T(8,128)} %shard_map.64) | data formatting | bytes 1048576

commit v3 on v2

v3 whole, which is shorter than its diff:
```python
import functools

import jax
import jax.numpy as jnp
from jax import lax
from jax.experimental import pallas as pl
from jax.experimental.pallas import tpu as pltpu
from jax.sharding import PartitionSpec as P

MESH = pl.DeviceIdType.MESH
LANES = 128
SLICES = 4
CHUNK = 32


def inner_size(col_count):
    inner = 1
    while inner * inner * 4 <= col_count and col_count % (inner * 2) == 0:
        inner *= 2
    return inner


def sorted_table(count):
    return [sorted(range(count), key=lambda d: (-abs(d - i), -abs(2 * d - count + 1), -d)) for i in range(count)]


def slots_of(size):
    return size + 1 if size > 2 else 1


def outer_first(packed):
    e = packed // 16
    return [(0, 0, 2 * e), (0, 8 * e, 4 * e), (1, 0, 5 * e)]


def inner_first(packed):
    e = packed // 16
    return [(0, 2 * e, 2 * e), (0, 4 * e, 4 * e), (0, 12 * e, 4 * e), (1, 5 * e, 3 * e), (1, 8 * e, 8 * e),
            (2, 0, 8 * e), (3, 0, 8 * e), (2, 8 * e, 8 * e), (3, 8 * e, 8 * e)]


def outer_second(packed):
    e = packed // 16
    return [(0, 2 * e, 6 * e, (0, 1)), (0, 12 * e, 4 * e, (2,)), (1, 5 * e, 11 * e, (3, 4)),
            (2, 0, 8 * e, (5,)), (3, 0, 8 * e, (6,)), (2, 8 * e, 8 * e, (7,)), (3, 8 * e, 8 * e, (8,))]


def kernel(
    dims,
    rows_hbm, cols_hbm, count_hbm, vec_hbm, deg_hbm, tiles_hbm, out_ref,
    rows_s, cols_s, count_s,
    tiles_v, vec_v, deg_v, fin, fout, gath, rhs, sums, part, inb, outb, zb, yb, prev_s, last_s,
    list_sem, tile_sem, vec_sem, deg_sem, d_send, d_recv, m_send, m_recv, f_send, f_recv,
    i_send, i_recv, o_send, o_recv, z_send, z_recv, y_send, y_recv,
):
    R, A, B, piece, width, side, slots = dims
    C = A * B
    S = SLICES
    gw = width // S
    packed = piece // S
    tpp = piece // side
    halves = S // tpp
    blocks = S
    grain = packed // blocks
    span = side // blocks
    Z = outer_first(packed)
    Y = inner_first(packed)
    O = outer_second(packed)
    chips = R // 2
    me_row = lax.axis_index("row")
    me_col = lax.axis_index("col")
    chip, core = me_row // 2, me_row % 2
    mate = chip * 2 + (1 - core)
    a, b = me_col // B, me_col % B
    f32 = jnp.float32

    def rdma(src, dst, ssem, rsem, where):
        return pltpu.make_async_remote_copy(
            src_ref=src, dst_ref=dst, send_sem=ssem, recv_sem=rsem,
            device_id=where, device_id_type=MESH,
        )

    vec_copy = pltpu.make_async_copy(vec_hbm, vec_v, vec_sem)
    vec_copy.start()
    deg_n = piece // LANES
    deg_at = (me_col * R + me_row, me_row * C + me_col)
    deg_copies = []
    for i, at in enumerate(deg_at):
        cp = pltpu.make_async_copy(
            deg_hbm.at[pl.ds(pl.multiple_of(at * deg_n, deg_n), deg_n)], deg_v.at[i], deg_sem.at[i])
        cp.start()
        deg_copies.append(cp)
    list_copies = []
    for i, (src, dst) in enumerate(((rows_hbm, rows_s), (cols_hbm, cols_s), (count_hbm, count_s))):
        cp = pltpu.make_async_copy(src, dst, list_sem.at[i])
        cp.start()
        list_copies.append(cp)
    tile_copy = pltpu.make_async_copy(tiles_hbm.at[0, 0], tiles_v, tile_sem)
    tile_copy.start()

    barrier = pltpu.get_barrier_semaphore()

    def greet(where):
        pl.semaphore_signal(barrier, inc=1, device_id=where, device_id_type=MESH)

    greet({"row": mate})
    for j in range(1, chips):
        greet({"row": lax.rem(chip + j, chips) * 2 + core})
    conds = []
    if B > 1:
        conds += [(b > 0, me_col - 1), (b < B - 1, me_col + 1)]
    if A > 1:
        conds += [(a > 0, me_col - B), (a < A - 1, me_col + B)]
    for cond, other in conds:
        @pl.when(cond)
        def _(other=other):
            greet({"col": other})
    peers = jnp.int32(chips)
    for cond, other in conds:
        peers = peers + jnp.where(cond, 1, 0)

    group = lax.broadcasted_iota(jnp.int32, (CHUNK, LANES), 1) // gw
    odd = group % 2 == 1

    def place(q):
        u, h = q // halves, q % halves
        return u, h

    def first_row(blk, h):
        return (blk * halves + h) * grain

    def by_group(values):
        out = values[S - 1]
        for g in range(S - 2, -1, -1):
            out = jnp.where(group == g, values[g], out)
        return out

    def roll(x, steps):
        steps = steps % S
        return pltpu.roll(x, steps * gw, 1) if steps else x

    for cp in deg_copies:
        cp.wait()
    for i, ref in enumerate((fin, fout)):
        f = lax.rsqrt(deg_v[i].astype(f32))
        lane_at = lax.broadcasted_iota(jnp.int32, f.shape, 1) // grain
        for m in range(packed // LANES):
            rows = []
            for q in range(S):
                u, h = place(q)
                row = jnp.zeros((1, LANES), f32)
                for w in range(LANES // grain):
                    node = u * side + first_row(m * (LANES // grain) + w, h)
                    shift = (w * grain - node) % LANES
                    g = pltpu.roll(f, shift, 1) if shift else f
                    at = node // LANES
                    row = jnp.where(lane_at[:1] == w, g[at:at + 1, :], row)
                rows.append(jnp.broadcast_to(row, (gw, LANES)))
            ref[m * LANES:(m + 1) * LANES, :] = jnp.concatenate(rows, 0).T

    def pack_own(s):
        for blk in range(blocks):
            for c in range(0, grain, CHUNK):
                v = []
                for q in range(S):
                    u, h = place(q)
                    at = u * side + first_row(blk, h) + c
                    v.append(roll(vec_v[at:at + CHUNK], q - s))
                to = blk * grain + c
                gath[s, me_row, to:to + CHUNK] = by_group(v) * fin[to:to + CHUNK]

    def send_own(s):
        for j in range(1, chips):
            dst = lax.rem(chip + j, chips) * 2 + core
            cp = rdma(gath.at[s, me_row], gath.at[s, me_row],
                      d_send.at[j - 1], d_recv.at[j - 1, s], {"row": dst})
            cp.start()
        cp = rdma(gath.at[s, me_row], gath.at[s, me_row],
                  m_send.at[0], m_recv.at[s], {"row": mate})
        cp.start()

    vec_copy.wait()
    pack_own(0)
    pl.semaphore_wait(barrier, peers)
    send_own(0)
    for s in range(1, S):
        pack_own(s)
        send_own(s)

    def link(k, _):
        rk = rows_s[0, 0, k]
        v = jnp.int32(slots)
        for j in range(slots):
            v = jnp.where((rows_s[0, 0, j] == rk) & (j < k), j, v)
        prev_s[k] = v
        return 0

    def ends(r, _):
        v = jnp.int32(slots)
        for j in range(slots):
            v = jnp.where((rows_s[0, 0, j] == r) & (j < count), j, v)
        last_s[r] = v
        return 0

    def landed(s, r, ssem, rsem):
        rdma(gath.at[s, r], gath.at[s, r], ssem, rsem, {"row": mate}).wait_recv()

    low = group < S // 2

    def operand(s, r, lane):
        for blk in range(blocks):
            for c in range(0, grain, CHUNK):
                at = blk * grain + c
                x = gath[s, r, at:at + CHUNK]
                hi = x.astype(jnp.bfloat16).astype(f32)
                lo = x - hi
                same, swapped = jnp.where(odd, lo, hi), jnp.where(odd, hi, lo)
                t = (same, roll(swapped, 1), roll(same, 2), roll(swapped, 3))
                e, f = jnp.where(odd, t[1], t[0]), jnp.where(odd, t[3], t[2])
                g, k = jnp.where(odd, t[0], t[3]), jnp.where(odd, t[2], t[1])
                spread = (jnp.where(low, e, f), jnp.where(low, g, k),
                          jnp.where(low, f, e), jnp.where(low, k, g))
                for q in range(S):
                    u, h = place(q)
                    to = first_row(blk, h) + c
                    rhs[r * tpp + u, to:to + CHUNK, lane:lane + LANES] = spread[q].astype(jnp.bfloat16)

    def forward(s):
        for j in range(1, chips):
            src = lax.rem(chip - j + chips, chips) * 2 + core
            landed(s, src, d_send.at[j - 1], d_recv.at[j - 1, s])
            cp = rdma(gath.at[s, src], gath.at[s, src],
                      f_send.at[j - 1], f_recv.at[j - 1, s], {"row": mate})
            cp.start()

    def arrivals(s):
        landed(s, mate, m_send.at[0], m_recv.at[s])
        for j in range(1, chips):
            src = lax.rem(chip - j + chips, chips) * 2 + (1 - core)
            landed(s, src, f_send.at[j - 1], f_recv.at[j - 1, s])

    def operands(s, lane):
        def step(r, _):
            operand(s, r, lane)
            return 0

        lax.fori_loop(0, R, step, 0)

    def products(blk, lanes):
        def product(k, _):
            both = jnp.dot(tiles_v[k, blk * span:(blk + 1) * span], rhs[cols_s[0, 0, k], :, :lanes],
                           preferred_element_type=f32)
            sums[k, :, :lanes] = both + sums[prev_s[k], :, :lanes]
            return 0

        lax.fori_loop(0, slots, product, 0, unroll=True)

    def pack(s, blk, lane):
        def step(dest, _):
            for c in range(0, grain, CHUNK):
                v = []
                for q in range(S):
                    u, h = place(q)
                    at = h * grain + c
                    v.append(sums[last_s[dest * tpp + u], at:at + CHUNK, lane:lane + LANES])
                x = by_group(v)
                y = by_group([v[(g + 1) % S] for g in range(S)])
                at = blk * grain + c
                part[s, dest, at:at + CHUNK] = x + roll(y, 1)
            return 0

        lax.fori_loop(0, C, step, 0, unroll=8)

    order = sorted_table(A)

    def pick(i):
        v = jnp.int32(order[0][i])
        for n in range(1, A):
            v = jnp.where(a == n, order[n][i], v)
        return v

    def line(pos, size, stride, dist, action):
        for right in (True, False):
            t = pos + dist if right else pos - dist
            slot = 0 if size <= 2 else t + 1 if right else t
            to = me_col + stride if right else me_col - stride
            more = pos > 0 if right else pos < size - 1

            @pl.when((t < size) if right else (t >= 0))
            def _(t=t, slot=slot, to=to, more=more):
                action(t, slot, to, more, dist < size - 1)

    def arrive(pos, size, ref, ssem, rsem, fold):
        if size > 1:
            for cond, slot in ((pos > 0, pos + 1), (pos < size - 1, pos)):
                slot = 0 if size <= 2 else slot

                @pl.when(cond)
                def _(slot=slot):
                    rdma(ref(slot), ref(slot), ssem(slot), rsem(slot), {"row": mate}).wait_recv()
        if size > 2:
            @pl.when((pos > 0) & (pos < size - 1))
            def _():
                fold(pos + 1, pos)

    near = jnp.where(b > 0, b + 1, 0) if B > 2 else 0
    near_a = jnp.where(a > 0, a + 1, 0) if A > 2 else 0

    def inner_copy(n, d, t, slot, to):
        s, lo, size = Y[n]
        at = pl.ds(lo, size)
        return rdma(part.at[s, d * B + t, at], inb.at[s, d, slot, at],
                    i_send.at[d, slot], i_recv.at[n, d, slot], {"col": to})

    def inner_send(n, i):
        d = pick(i)
        s, lo, size = Y[n]
        at = pl.ds(lo, size)

        def action(t, slot, to, more, can):
            cp = inner_copy(n, d, t, slot, to)
            if can:
                @pl.when(more)
                def _():
                    cp.wait_recv()
                    part[s, d * B + t, at] = part[s, d * B + t, at] + inb[s, d, slot, at]
            cp.start()

        for dist in range(B - 1, 0, -1):
            line(b, B, 1, dist, action)

    def inner_done(n, d):
        s, lo, size = Y[n]
        at = pl.ds(lo, size)

        def fold(x, y):
            inb[s, d, x, at] = inb[s, d, x, at] + inb[s, d, y, at]

        arrive(b, B, lambda q: inb.at[s, d, q, at], lambda q: i_send.at[d, q],
               lambda q: i_recv.at[n, d, q], fold)

    def here(s, d, at):
        v = part[s, d * B + b, at]
        if B > 1:
            v = v + inb[s, d, near, at]
        return v

    def outer_copy(n, i):
        s, lo, size, _ = O[n]
        at = pl.ds(lo, size)
        d = pick(i)
        right = d > a
        slot = jnp.where(right, d + 1, d) if A > 2 else 0
        to = jnp.where(right, me_col + B, me_col - B)
        more = (right & (a > 0)) | (jnp.logical_not(right) & (a < A - 1))
        cp = rdma(part.at[s, d * B + b, at], outb.at[s, slot, at],
                  o_send.at[slot], o_recv.at[n, slot], {"col": to})
        return d, slot, more, cp

    def outer_now(n, i):
        d, slot, more, cp = outer_copy(n, i)
        s, lo, size, parts = O[n]
        at = pl.ds(lo, size)

        @pl.when(jnp.logical_not(more))
        def _():
            for p in parts:
                inner_done(p, d)
            part[s, d * B + b, at] = here(s, d, at)
            cp.start()

    def outer_later(n, i):
        d, slot, more, cp = outer_copy(n, i)
        s, lo, size, parts = O[n]
        at = pl.ds(lo, size)

        @pl.when(more)
        def _():
            for p in parts:
                inner_done(p, d)
            cp.wait_recv()
            part[s, d * B + b, at] = here(s, d, at) + outb[s, slot, at]
            cp.start()

    def tail_copy(n, d, slot, to):
        s, lo, size = Z[n]
        return rdma(part.at[s, pl.ds(d * B, B), pl.ds(lo, size)], zb.at[n, slot, :, pl.ds(0, size)],
                    z_send.at[slot], z_recv.at[n, slot], {"col": to})

    def tail_now(n):
        def action(d, slot, to, more, can):
            cp = tail_copy(n, d, slot, to)

            @pl.when(jnp.logical_not(more))
            def _():
                cp.start()

        for dist in range(A - 1, 0, -1):
            line(a, A, B, dist, action)

    def tail_later(n, dists):
        s, lo, size = Z[n]

        def action(d, slot, to, more, can):
            cp = tail_copy(n, d, slot, to)

            @pl.when(more)
            def _():
                cp.wait_recv()
                for t in range(B):
                    at = pl.ds(lo, size)
                    part[s, d * B + t, at] = part[s, d * B + t, at] + zb[n, slot, t, :size]
                cp.start()

        for dist in dists:
            line(a, A, B, dist, action)

    def turn_copy(n, t, slot, to):
        s, lo, size = Z[n]
        return rdma(part.at[s, a * B + t, pl.ds(lo, size)], yb.at[n, slot, pl.ds(0, size)],
                    y_send.at[slot], y_recv.at[n, slot], {"col": to})

    def turn(n):
        s, lo, size = Z[n]
        at = pl.ds(lo, size)

        def fold(x, y):
            zb[n, x, :, :size] = zb[n, x, :, :size] + zb[n, y, :, :size]

        arrive(a, A, lambda q: zb.at[n, q, :, pl.ds(0, size)], lambda q: z_send.at[q],
               lambda q: z_recv.at[n, q], fold)

        def action(t, slot, to, more, can):
            cp = turn_copy(n, t, slot, to)
            v = part[s, a * B + t, at]
            if A > 1:
                v = v + zb[n, near_a, t, :size]
            part[s, a * B + t, at] = v
            if can:
                @pl.when(more)
                def _():
                    cp.wait_recv()
                    part[s, a * B + t, at] = part[s, a * B + t, at] + yb[n, slot, :size]
            cp.start()

        for dist in range(B - 1, 0, -1):
            line(b, B, 1, dist, action)

    def write(s, lo, size, get):
        step = 16
        for at in range(lo, lo + size, step):
            blk, c = at // grain, at % grain
            total = get(at, step) * fout[at:at + step]
            for q in range(S):
                u, h = place(q)
                to = u * side + first_row(blk, h) + c
                out_ref[to:to + step, s * gw:(s + 1) * gw] = roll(total, s - q)[:, s * gw:(s + 1) * gw]

    def finish(n):
        s, lo, size, parts = O[n]
        at = pl.ds(lo, size)
        for p in parts:
            inner_done(p, a)
        if A > 1:
            def fold(x, y):
                outb[s, x, at] = outb[s, x, at] + outb[s, y, at]

            arrive(a, A, lambda q: outb.at[s, q, at], lambda q: o_send.at[q],
                   lambda q: o_recv.at[n, q], fold)

        def get(first, step):
            v = here(s, a, pl.ds(first, step))
            if A > 1:
                v = v + outb[s, near_a, first:first + step]
            return v

        write(s, lo, size, get)

    def finish_tail(n):
        s, lo, size = Z[n]

        def fold(x, y):
            yb[n, x, :size] = yb[n, x, :size] + yb[n, y, :size]

        arrive(b, B, lambda q: yb.at[n, q, pl.ds(0, size)], lambda q: y_send.at[q],
               lambda q: y_recv.at[n, q], fold)

        def get(first, step):
            v = part[s, a * B + b, first:first + step]
            at = first - lo
            if A > 1:
                v = v + zb[n, near_a, b, at:at + step]
            if B > 1:
                v = v + yb[n, near, at:at + step]
            return v

        write(s, lo, size, get)

    for cp in list_copies:
        cp.wait()
    count = count_s[0, 0]
    lax.fori_loop(0, slots, link, 0)
    lax.fori_loop(0, C * tpp, ends, 0)
    sums[slots] = jnp.zeros((span, 2 * LANES), f32)

    every = range(A)
    hops = range(A - 1)

    def inner_all(n):
        for i in every:
            inner_send(n, i)

    operand(0, me_row, 0)
    landed(0, mate, m_send.at[0], m_recv.at[0])
    operand(0, mate, 0)
    forward(0)
    for j in range(1, chips):
        operand(0, lax.rem(chip - j + chips, chips) * 2 + core, 0)
    for j in range(1, chips):
        src = lax.rem(chip - j + chips, chips) * 2 + (1 - core)
        landed(0, src, f_send.at[j - 1], f_recv.at[j - 1, 0])
        operand(0, src, 0)
    tile_copy.wait()
    def block(blk, lanes, first):
        products(blk, lanes)
        for n in range(lanes // LANES):
            pack(first + n, blk, n * LANES)

    block(0, LANES, 0)
    tail_now(0)
    inner_all(0)
    block(1, LANES, 0)
    inner_all(1)
    forward(1)
    block(2, LANES, 0)
    tail_now(1)
    block(3, LANES, 0)
    inner_all(2)
    forward(2)
    arrivals(1)
    operands(1, 0)
    block(0, LANES, 1)
    block(1, LANES, 1)
    tail_now(2)
    inner_all(3)
    block(2, LANES, 1)
    block(3, LANES, 1)
    inner_all(4)
    forward(3)
    far, near_hop = range(A - 2, 1, -1), range(min(1, A - 2), 0, -1)
    tail_later(0, far)
    for i in hops:
        outer_now(0, i)
    tail_later(1, far)
    for s in (2, 3):
        arrivals(s)
        operands(s, (s - 2) * LANES)
    for i in hops:
        outer_now(1, i)
    tail_later(0, near_hop)
    tail_later(1, near_hop)
    tail_later(2, far)
    block(0, 2 * LANES, 2)
    block(1, 2 * LANES, 2)
    inner_send(5, 0)
    inner_send(6, 0)
    block(2, 2 * LANES, 2)
    block(3, 2 * LANES, 2)
    inner_send(7, 0)
    inner_send(8, 0)
    for i in range(1, A):
        for n in (5, 6, 7, 8):
            inner_send(n, i)
    tail_later(2, near_hop)
    for i in hops:
        outer_now(2, i)
    for n in (0, 1, 2):
        for i in list(range(A - 3)) + list(range(A - 2, max(A - 4, -1), -1)):
            outer_later(n, i)
    last = (3, 4, 5, 6)
    now = [(n, i) for i in hops for n in last]
    later = sorted(now, key=lambda v: (max(v[1] - (A - 4), 0) * 2 + 0.1 * v[1] + 4 * min(v[1], A - 4) + last.index(v[0])))
    for k, (x, y) in enumerate(zip(now, later)):
        outer_now(*x)
        outer_later(*y)
        if k == 3:
            for n in range(len(Z)):
                turn(n)
            finish(0)
            finish(1)
        if k == 7:
            finish(2)
    for n in last:
        finish(n)
    for n in range(len(Z)):
        finish_tail(n)

    def all_sent(rows, sem):
        at = out_ref.at[pl.ds(0, rows)]
        rdma(at, at, sem, sem, {"row": mate}).wait_send()

    for j in range(1, chips):
        all_sent(piece, d_send.at[j - 1])
        all_sent(piece, f_send.at[j - 1])
    all_sent(piece, m_send.at[0])
    turned = sum(size for _, _, size in Z)
    for dist in range(A - 1, 0, -1):
        line(a, A, B, dist, lambda d, slot, *rest: all_sent(B * turned, z_send.at[slot]))
    for dist in range(B - 1, 0, -1):
        line(b, B, 1, dist, lambda t, slot, *rest: all_sent(turned, y_send.at[slot]))
    for d in range(A):
        for dist in range(B - 1, 0, -1):
            line(b, B, 1, dist, lambda t, slot, *rest, d=d: all_sent(piece - turned, i_send.at[d, slot]))
    for dist in range(A - 1, 0, -1):
        line(a, A, B, dist, lambda d, slot, *rest: all_sent(piece - turned, o_send.at[slot]))


def body(vectors, tile_values, tile_rows, tile_cols, tile_count, degrees):
    R = lax.axis_size("row")
    C = lax.axis_size("col")
    piece, width = vectors.shape
    side = tile_values.shape[-1]
    slots = tile_values.shape[2]
    B = inner_size(C)
    A = C // B
    tpp = piece // side
    chips = R // 2
    dims = (R, A, B, piece, width, side, slots)
    vmem = pl.BlockSpec(memory_space=pltpu.VMEM)
    anywhere = pl.BlockSpec(memory_space=pl.ANY)
    dma = pltpu.SemaphoreType.DMA
    f32 = jnp.float32
    far = max(chips - 1, 1)
    S = SLICES
    packed = piece // S
    Z, Y = outer_first(packed), inner_first(packed)
    NO = len(outer_second(packed))
    along, over = slots_of(A), slots_of(B)
    NZ, NY, longest = len(Z), len(Y), max(n for _, _, n in Z)
    smem_i32 = lambda *shape: pltpu.SMEM(shape, jnp.int32)
    return pl.pallas_call(
        functools.partial(kernel, dims),
        out_shape=jax.ShapeDtypeStruct((piece, width), f32),
        in_specs=[anywhere] * 6,
        out_specs=vmem,
        scratch_shapes=[
            smem_i32(1, 1, slots), smem_i32(1, 1, slots), smem_i32(1, 1),
            pltpu.VMEM((slots, side, side), tile_values.dtype),
            pltpu.VMEM((piece, width), f32),
            pltpu.VMEM((2, piece // LANES, LANES), jnp.int32),
            pltpu.VMEM((packed, LANES), f32),
            pltpu.VMEM((packed, LANES), f32),
            pltpu.VMEM((S, R, packed, LANES), f32),
            pltpu.VMEM((R * tpp, side, 2 * LANES), jnp.bfloat16),
            pltpu.VMEM((slots + 1, side // S, 2 * LANES), f32),
            pltpu.VMEM((S, C, packed, LANES), f32),
            pltpu.VMEM((S, A, over, packed, LANES), f32),
            pltpu.VMEM((S, along, packed, LANES), f32),
            pltpu.VMEM((NZ, along, B, longest, LANES), f32),
            pltpu.VMEM((NZ, over, longest, LANES), f32),
            smem_i32(slots), smem_i32(C * tpp),
            dma((3,)), dma, dma, dma((2,)),
            dma((far,)), dma((far, S)),
            dma((1,)), dma((S,)),
            dma((far,)), dma((far, S)),
            dma((A, over)), dma((NY, A, over)),
            dma((along,)), dma((NO, along)),
            dma((along,)), dma((NZ, along)),
            dma((over,)), dma((NZ, over)),
        ],
        compiler_params=pltpu.CompilerParams(
            collective_id=0, has_side_effects=True, vmem_limit_bytes=67043328
        ),
    )(tile_rows, tile_cols, tile_count, vectors, degrees.reshape(-1, LANES), tile_values)


def solution(mesh):
    placed = (
        P(("col", "row"), None),
        P("row", "col", None, None, None),
        P("row", "col", None),
        P("row", "col", None),
        P("row", "col"),
        P(),
    )
    return jax.shard_map(
        body, mesh=mesh, in_specs=placed, out_specs=P(("row", "col"), None), check_vma=False
    )
```

time: 62.7 us -> 59.2 us (0.944)
  Pallas kernels: 60 us -> 56.5 us
    pallas_call x1, Pallas kernels: 60 us -> 56.5 us  [body(): pl.pallas_call(functools.partial(kernel, dims), out_shape=jax.ShapeDtypeS...]
where the time goes in v3:
time: 59.2 us; the launch traced here: 59.1 us
  Pallas kernels  56.5 us (95%)
  local copies, waits for them, and re-layouts  1.87 us (3%)
  between operations  0.66 us (1%)
    pallas_call x1, Pallas kernels, body(): pl.pallas_call(functools.partial(kernel, dims), out_shape=jax.ShapeDtypeS...  56.5 us
    unnamed x1, local copies, waits for them, and re-layouts  1.87 us

profile of v3, /device:TPU:0, one launch (start us, length us, event | category | flops | bytes accessed | tf_op | source)
XLA Modules:
  0.0 59.1 jit_solution(6247006909205113900)
XLA Ops:
  0.7 56.5 %shard_map.64 = f32[1024,128]{1,0:T(8,128)} custom-call(s32[1,1,22]{2,1,0:T(1,128)} %rows_hbm.1, s32[1,1,22]{2,1,0:T(1,128)} %cols_hbm.1, s32[1,1]{1,0:T(1,128)S(6)} %copy.8.count_hbm, f32[1024,128]{1,0:T(8,128)} %vec_hbm.1, s32[256,128]{1,0:T(8,128)} %bitcast.1, bf16[1,1,22,512,512]{4,3,2,1,0:T(8,128)(2,1)} %tiles_hbm.1), custom_call_target="tpu_custom_call" | custom-call | tf_op jit(solution)/shard_map/pallas_call | solution.py:641
  57.2 1.9 %copy.9 = f32[1024,128]{1,0:T(8,128)} copy(f32[1024,128]{1,0:T(8,128)} %shard_map.64) | data formatting | bytes 1048576

commit v4 on v3

--- a/solution.py
+++ b/solution.py
@@ -30,18 +30,18 @@
 
 def outer_first(packed):
     e = packed // 16
-    return [(0, 0, 2 * e), (0, 8 * e, 4 * e), (1, 0, 5 * e)]
+    return [(0, 0, 2 * e), (0, 8 * e, 4 * e), (1, 0, 4 * e)]
 
 
 def inner_first(packed):
     e = packed // 16
-    return [(0, 2 * e, 2 * e), (0, 4 * e, 4 * e), (0, 12 * e, 4 * e), (1, 5 * e, 3 * e), (1, 8 * e, 8 * e),
+    return [(0, 2 * e, 2 * e), (0, 4 * e, 4 * e), (0, 12 * e, 4 * e), (1, 4 * e, 4 * e), (1, 8 * e, 8 * e),
             (2, 0, 8 * e), (3, 0, 8 * e), (2, 8 * e, 8 * e), (3, 8 * e, 8 * e)]
 
 
 def outer_second(packed):
     e = packed // 16
-    return [(0, 2 * e, 6 * e, (0, 1)), (0, 12 * e, 4 * e, (2,)), (1, 5 * e, 11 * e, (3, 4)),
+    return [(0, 2 * e, 6 * e, (0, 1)), (0, 12 * e, 4 * e, (2,)), (1, 4 * e, 12 * e, (3, 4)),
             (2, 0, 8 * e, (5,)), (3, 0, 8 * e, (6,)), (2, 8 * e, 8 * e, (7,)), (3, 8 * e, 8 * e, (8,))]
 
 
@@ -557,13 +557,13 @@
         operands(s, (s - 2) * LANES)
     for i in hops:
         outer_now(1, i)
-    tail_later(0, near_hop)
-    tail_later(1, near_hop)
-    tail_later(2, far)
     block(0, 2 * LANES, 2)
     block(1, 2 * LANES, 2)
     inner_send(5, 0)
     inner_send(6, 0)
+    tail_later(0, near_hop)
+    tail_later(1, near_hop)
+    tail_later(2, far)
     block(2, 2 * LANES, 2)
     block(3, 2 * LANES, 2)
     inner_send(7, 0)

time: 59.2 us -> 57.6 us (0.973)
  Pallas kernels: 56.5 us -> 54.9 us
    pallas_call x1, Pallas kernels: 56.5 us -> 54.9 us  [body(): pl.pallas_call(functools.partial(kernel, dims), out_shape=jax.ShapeDtypeS...]
where the time goes in v4:
time: 57.6 us; the launch traced here: 57.4 us
  Pallas kernels  54.9 us (95%)
  local copies, waits for them, and re-layouts  1.87 us (3%)
  between operations  0.66 us (1%)
    pallas_call x1, Pallas kernels, body(): pl.pallas_call(functools.partial(kernel, dims), out_shape=jax.ShapeDtypeS...  54.9 us
    unnamed x1, local copies, waits for them, and re-layouts  1.87 us

profile of v4, /device:TPU:0, one launch (start us, length us, event | category | flops | bytes accessed | tf_op | source)
XLA Modules:
  0.0 57.4 jit_solution(13133273801828844151)
XLA Ops:
  0.7 54.9 %shard_map.64 = f32[1024,128]{1,0:T(8,128)} custom-call(s32[1,1,22]{2,1,0:T(1,128)} %rows_hbm.1, s32[1,1,22]{2,1,0:T(1,128)} %cols_hbm.1, s32[1,1]{1,0:T(1,128)S(6)} %copy.8.count_hbm, f32[1024,128]{1,0:T(8,128)} %vec_hbm.1, s32[256,128]{1,0:T(8,128)} %bitcast.1, bf16[1,1,22,512,512]{4,3,2,1,0:T(8,128)(2,1)} %tiles_hbm.1), custom_call_target="tpu_custom_call" | custom-call | tf_op jit(solution)/shard_map/pallas_call | solution.py:641
  55.6 1.9 %copy.9 = f32[1024,128]{1,0:T(8,128)} copy(f32[1024,128]{1,0:T(8,128)} %shard_map.64) | data formatting | bytes 1048576

commit v5 on v4

--- a/solution.py
+++ b/solution.py
@@ -574,21 +574,21 @@
     tail_later(2, near_hop)
     for i in hops:
         outer_now(2, i)
-    for n in (0, 1, 2):
-        for i in list(range(A - 3)) + list(range(A - 2, max(A - 4, -1), -1)):
-            outer_later(n, i)
+    lag = lambda i: 0.3 if i == A - 2 else 1.2 if i == A - 3 else 0
+    for n, i in sorted(((n, i) for n in (0, 1, 2) for i in hops), key=lambda v: v[0] + lag(v[1])):
+        outer_later(n, i)
     last = (3, 4, 5, 6)
     now = [(n, i) for i in hops for n in last]
     later = sorted(now, key=lambda v: (max(v[1] - (A - 4), 0) * 2 + 0.1 * v[1] + 4 * min(v[1], A - 4) + last.index(v[0])))
     for k, (x, y) in enumerate(zip(now, later)):
         outer_now(*x)
         outer_later(*y)
-        if k == 3:
+        if k == 6:
             for n in range(len(Z)):
                 turn(n)
             finish(0)
             finish(1)
-        if k == 7:
+        if k == 9:
             finish(2)
     for n in last:
         finish(n)

time: 57.6 us -> 57.6 us (level)
  no operation moved by 1% of the time
where the time goes in v5:
time: 57.6 us; the launch traced here: 57.4 us
  Pallas kernels  54.9 us (95%)
  local copies, waits for them, and re-layouts  1.87 us (3%)
  between operations  0.66 us (1%)
    pallas_call x1, Pallas kernels, body(): pl.pallas_call(functools.partial(kernel, dims), out_shape=jax.ShapeDtypeS...  54.9 us
    unnamed x1, local copies, waits for them, and re-layouts  1.87 us

profile of v5, /device:TPU:0, one launch (start us, length us, event | category | flops | bytes accessed | tf_op | source)
XLA Modules:
  0.0 57.4 jit_solution(15137541066022206585)
XLA Ops:
  0.7 54.9 %shard_map.64 = f32[1024,128]{1,0:T(8,128)} custom-call(s32[1,1,22]{2,1,0:T(1,128)} %rows_hbm.1, s32[1,1,22]{2,1,0:T(1,128)} %cols_hbm.1, s32[1,1]{1,0:T(1,128)S(6)} %copy.8.count_hbm, f32[1024,128]{1,0:T(8,128)} %vec_hbm.1, s32[256,128]{1,0:T(8,128)} %bitcast.1, bf16[1,1,22,512,512]{4,3,2,1,0:T(8,128)(2,1)} %tiles_hbm.1), custom_call_target="tpu_custom_call" | custom-call | tf_op jit(solution)/shard_map/pallas_call | solution.py:641
  55.6 1.9 %copy.9 = f32[1024,128]{1,0:T(8,128)} copy(f32[1024,128]{1,0:T(8,128)} %shard_map.64) | data formatting | bytes 1048576
